TPU v7x, 256 devices: a whole 4x4x8 slice. The times are simulated.
256 devices in a mesh: list: 32 (over x, y, core), rep: 8 (over z).
Axes of the slice: x: 4, y: 4, z: 8, core: 2. Of those that a mesh axis runs over, the one named last changes fastest.
Arguments:
- memory_rows: bfloat16 [65536, 1024], P(('list', 'rep'))
- list_owner: int32 [65536, 1], P(('list', 'rep')), may hold values from 0 to 31; in each aligned block of 256 rows (0 to 255, 256 to 511, ...) at most 32 rows name the same one
- list_slot: int32 [65536], P(('list', 'rep')), may hold values from 0 to 2047
- pq_codes: int32 [65536, 16], P(('list', 'rep')), may hold values from 0 to 255
- valid_rows: int32 [256], P(('list', 'rep')), may hold values from 128 to 256
- centroids: bfloat16 [65536, 1024], P('list'), may hold values from -3 to 3
- codebook: float32 [16, 256, 64], replicated
Outputs:
- new_codebook: float32 [16, 256, 64], P('rep')
- row_error: float32 [65536], P(('list', 'rep'))
Inputs may be any that keep to these rules, and one draw needn't show every extreme that they name: `list_owner`: the rows of one device name one index of list at most 32 times, and some device's rows name one exactly 32 times.
All inputs are finite; a program needn't handle non-finite values.
Results may differ from a plain program's by a relative error of at most 0.0038.
Values may be sent and summed in bfloat16 or wider, within the bound.
A program may use at most 128 MiB of HBM per device.

v0:
```python
import jax
import jax.numpy as jnp
from jax import lax
from jax.sharding import PartitionSpec as P

prior_weight = 4.0


def code_statistics(residual, pq_codes, is_live, codebook):
    row_count = residual.shape[0]
    subspaces = codebook.shape[0]
    code_count = codebook.shape[1]
    width_sub = codebook.shape[2]
    residual = jnp.where(is_live[:, None], residual, 0.0)
    recon = codebook[jnp.arange(subspaces)[None, :], pq_codes].reshape(
        row_count, subspaces * width_sub
    )
    row_error = jnp.where(is_live, jnp.mean((residual - recon) ** 2, axis=1), 0.0)
    rounded = (
        residual.astype(jnp.bfloat16).reshape(row_count, subspaces, width_sub).transpose(1, 0, 2)
    )
    codes_major = pq_codes.T

    def per_subspace(item):
        code_col, part_rows = item
        onehot = ((code_col[:, None] == jnp.arange(code_count)[None, :]) & is_live[:, None]).astype(
            jnp.bfloat16
        )
        sums_one = lax.dot_general(
            onehot, part_rows, (((0,), (0,)), ((), ())), preferred_element_type=jnp.float32
        )
        counts_one = jnp.sum(onehot.astype(jnp.float32), axis=0)
        return (sums_one, counts_one)

    sums, counts = lax.map(per_subspace, (codes_major, rounded))
    return (row_error, sums, counts)


def body(memory_rows, list_owner, list_slot, pq_codes, valid_rows, centroids, codebook):
    row_count = memory_rows.shape[0]
    width = memory_rows.shape[1]
    list_count = centroids.shape[0]
    owners = lax.axis_size("list")
    capacity = 4 * row_count // owners
    is_valid = jnp.arange(row_count) < valid_rows[0]
    target = list_owner[:, 0]
    onehot_dest = ((target[:, None] == jnp.arange(owners)[None, :]) & is_valid[:, None]).astype(
        jnp.int32
    )
    before = jnp.cumsum(onehot_dest, axis=0) - onehot_dest
    slot_rank = jnp.sum(before * onehot_dest, axis=1)
    position = jnp.where(is_valid, target * capacity + slot_rank, owners * capacity)
    taken = jnp.clip(position, 0, owners * capacity - 1)
    total_slots = owners * capacity
    send_rows = (
        jnp.zeros((total_slots, width), jnp.bfloat16).at[position].set(memory_rows, mode="drop")
    )
    send_slot = jnp.full((total_slots,), -1, jnp.int32).at[position].set(list_slot, mode="drop")
    send_codes = (
        jnp.zeros((total_slots, pq_codes.shape[1]), jnp.int32)
        .at[position]
        .set(pq_codes, mode="drop")
    )
    got_rows, got_slot, got_codes = (
        lax.all_to_all(
            send_rows.reshape(owners, capacity, width),
            "list",
            split_axis=0,
            concat_axis=0,
            tiled=True,
        ),
        lax.all_to_all(
            send_slot.reshape(owners, capacity), "list", split_axis=0, concat_axis=0, tiled=True
        ),
        lax.all_to_all(
            send_codes.reshape(owners, capacity, pq_codes.shape[1]),
            "list",
            split_axis=0,
            concat_axis=0,
            tiled=True,
        ),
    )
    got_rows = got_rows.reshape(total_slots, width)
    got_slot = got_slot.reshape(total_slots)
    got_codes = got_codes.reshape(total_slots, pq_codes.shape[1])
    is_live = got_slot >= 0
    centre = centroids[jnp.clip(got_slot, 0, list_count - 1)].astype(jnp.float32)
    residual = got_rows.astype(jnp.float32) - centre
    slot_error, sums, counts = code_statistics(residual, got_codes, is_live, codebook)
    returned = lax.all_to_all(
        slot_error.reshape(owners, capacity), "list", split_axis=0, concat_axis=0, tiled=True
    )
    row_error = jnp.where(is_valid, returned.reshape(total_slots)[taken], 0.0)
    subspaces = codebook.shape[0]
    replicas = lax.axis_size("rep")
    share = subspaces // replicas
    first_sub = lax.axis_index("rep") * share
    sums_all, counts_all = lax.psum((sums, counts), ("list", "rep"))
    sums_mine = lax.dynamic_slice_in_dim(sums_all, first_sub, share, 0)
    counts_mine = lax.dynamic_slice_in_dim(counts_all, first_sub, share, 0)
    old_mine = lax.dynamic_slice_in_dim(codebook, first_sub, share, 0)
    new_codebook = (sums_mine + prior_weight * old_mine) / (counts_mine[:, :, None] + prior_weight)
    return (new_codebook, row_error)


def solution(mesh):
    in_specs = (
        P(("list", "rep"), None),
        P(("list", "rep"), None),
        P(("list", "rep")),
        P(("list", "rep"), None),
        P(("list", "rep")),
        P("list", None),
        P(),
    )
    out_specs = (P("rep", None, None), P(("list", "rep")))
    return jax.shard_map(body, mesh=mesh, in_specs=in_specs, out_specs=out_specs, check_vma=False)
```

profile of v0, /device:TPU:1, one launch (start us, length us, event | category | flops | bytes accessed | tf_op | source)
XLA Modules:
  0.0 581.5 jit_solution(2420515403371690203)
XLA Ops:
  13.1 8.6 %all-to-all-start.1 = ((s32[32,1,32]{2,1,0:T(1,128)}), s32[32,1,32]{2,1,0:T(1,128)S(1)}, u32[]{:S(2)}, u32[]{:S(2)}) async-start(s32[32,1,32]{2,1,0:T(1,128)} %all_to_all.17), calls=%async_computation.1 | async-start | bytes 32768 | tf_op jit(solution)/shard_map/all_to_all | solution.py:72
  24.8 3.8 all-to-all-done.1
  28.7 4.2 all-to-all-start
  32.8 3.7 scatter_custom_fusion.2
  36.6 3.8 all-to-all-done
  40.3 4.8 all-to-all-start.2
  46.1 8.8 %gather_fusion = bf16[1024,1024]{1,0:T(8,128)(2,1)} fusion(bf16[2048,1024]{1,0:T(8,128)(2,1)} %param.14, s32[1024]{0:T(1024)S(1)} %broadcast_clamp_fusion.1), kind=kCustom, calls=%fused_computation | custom fusion | bytes 4198400 | tf_op jit(solution)/shard_map/gather | solution.py:87
  54.8 4.1 copy.44
  58.9 4.0 convert_element_type.53
  62.9 8.1 %copy.45 = f32[1024,16,64]{2,1,0:T(8,128)} copy(f32[1024,16,64]{0,2,1:T(8,128)} %bitcast.73) | data formatting | bytes 8388608 | tf_op jit(solution)/shard_map/convert_element_type | solution.py:87
  73.4 176.0 %gather_fusion.1 = f32[16384,64]{1,0:T(8,128)} fusion(f32[16,256,64]{2,1,0:T(8,128)S(1)} %copy.49, s32[16384]{0:T(1024)S(1)} %reshape.188), kind=kCustom, calls=%fused_computation.1 | custom fusion | bytes 8519680 | tf_op jit(solution)/shard_map/gather | solution.py:15
  249.4 7.6 %gather.13 = f32[32,32,1024]{2,1,0:T(8,128)} reshape(f32[16384,64]{1,0:T(8,128)} %gather_fusion.1) | data formatting | bytes 8388608 | tf_op jit(solution)/shard_map/gather | solution.py:15
  257.0 6.9 %reshape.177 = f32[1024,16,64]{2,1,0:T(8,128)} reshape(bf16[32,32,1024]{2,1,0:T(8,128)(2,1)} %all-to-all-done.2) | data formatting | bytes 6291456 | tf_op jit(solution)/shard_map/convert_element_type | solution.py:88
  263.8 7.7 %fusion.9 = bf16[16,1024,64]{2,0,1:T(8,128)(2,1)S(1)} fusion(f32[1024,16,64]{2,1,0:T(8,128)} %reshape.177, f32[1024,16,64]{2,1,0:T(8,128)} %copy.45, pred[1024]{0:T(1024)(128)(4,1)S(1)} %ge.17), kind=kLoop, calls=%fused_computation.19 | loop fusion | flops 3145728 | bytes 10486784 | tf_op jit(solution)/shard_map/transpose | solution.py:20
  271.6 3.0 copy.46
  274.6 40.9 %while.12 = (s32[]{:T(128)}, f32[16,256,64]{1,2,0:T(8,128)}, f32[16,256]{1,0:T(8,128)S(1)}, s32[16,1024]{1,0:T(8,128)S(1)}, pred[1024]{0:T(1024)(128)(4,1)S(1)},...) while((s32[]{:T(128)}, f32[16,256,64]{1,2,0:T(8,128)}, f32[16,256]{1,0:T(8,128)S(1)}, ...), condition=%wide.region_8.9_spmd, body=%wide.region_6.8_spmd.sunk | while | flops 35389184 | bytes 350301 | solution.py:35
  277.1 2.1 fusion.31
  279.7 2.1 fusion.31
  295.0 2.1 fusion.31
  312.9 2.1 fusion.31
  315.5 5.1 multiply_reduce_fusion
  321.2 7.5 %all-to-all-start.3 = ((f32[32,1,32]{2,1,0:T(1,128)}), f32[32,1,32]{2,1,0:T(1,128)S(1)}, u32[]{:S(2)}, u32[]{:S(2)}) async-start(f32[32,1,32]{2,1,0:T(1,128)} %bitcast.21), calls=%async_computation.3 | async-start | bytes 32768 | tf_op jit(solution)/shard_map/all_to_all | solution.py:90
  328.7 81.7 %psum.15 = f32[16,256]{1,0:T(8,128)S(1)} all-reduce(f32[16,256]{1,0:T(8,128)S(1)} %get-tuple-element.36), channel_id=1, replica_groups=mesh['list'=32,'rep'=8] {'list','rep'}, use_global_device_ids=true, to_apply=%region_10.11 | all-reduce | flops 4096 | bytes 32768 | tf_op jit(solution)/shard_map/psum | solution.py:98
  413.6 159.4 %all-reduce.2.cloned.1.call-done = f32[16,256,64]{1,2,0:T(8,128)} async-done(((f32[16,256,64]{1,2,0:T(8,128)}), f32[16,256,64]{1,2,0:T(8,128)}) %all-reduce.2.cloned.1.call-update) | async-done | bytes 1048592 | tf_op jit(solution)/shard_map/psum | solution.py:98
  (110 shorter events, 49.0 us)
Async XLA Ops:
  9.1 36.2 %copy-start = (f32[16,256,64]{1,2,0:T(8,128)S(1)}, f32[16,256,64]{1,2,0:T(8,128)}, u32[]{:S(2)}) copy-start(f32[16,256,64]{1,2,0:T(8,128)} %param.15) | copy-start | bytes 3145732
  13.1 15.5 %all-to-all-start.1 = ((s32[32,1,32]{2,1,0:T(1,128)}), s32[32,1,32]{2,1,0:T(1,128)S(1)}, u32[]{:S(2)}, u32[]{:S(2)}) async-start(s32[32,1,32]{2,1,0:T(1,128)} %all_to_all.17), calls=%async_computation.1 | async-start | bytes 32768 | tf_op jit(solution)/shard_map/all_to_all | solution.py:72
  28.7 11.7 %all-to-all-start = ((s32[32,1,512]{2,1,0:T(1,128)}), s32[32,1,512]{2,1,0:T(1,128)S(1)}, u32[]{:S(2)}, u32[]{:S(2)}) async-start(s32[32,1,512]{2,1,0:T(1,128)} %reshape.243), calls=%async_computation | async-start | bytes 131072 | tf_op jit(solution)/shard_map/all_to_all | solution.py:75
  40.3 216.7 %all-to-all-start.2 = ((bf16[32,32,1024]{2,1,0:T(8,128)(2,1)}), bf16[32,32,1024]{2,1,0:T(8,128)(2,1)}, u32[]{:S(2)}, u32[]{:S(2)}) async-start(bf16[32,32,1024]{2,1,0:T(8,128)(2,1)} %bitcast.13), calls=%async_computation.2 | async-start | bytes 4194304 | tf_op jit(solution)/shard_map/all_to_all | solution.py:65
  45.1 527.9 %all-reduce.2.cloned.1.call-start = ((), (), s32[]{:S(2)}) async-start(), calls=%async_computation.4 | async-start | bytes 2097152 | tf_op jit(solution)/shard_map/psum | solution.py:98
  321.2 89.2 %all-to-all-start.3 = ((f32[32,1,32]{2,1,0:T(1,128)}), f32[32,1,32]{2,1,0:T(1,128)S(1)}, u32[]{:S(2)}, u32[]{:S(2)}) async-start(f32[32,1,32]{2,1,0:T(1,128)} %bitcast.21), calls=%async_computation.3 | async-start | bytes 32768 | tf_op jit(solution)/shard_map/all_to_all | solution.py:90
Sparse Core Ops, SparseCore 0:
  315.6 257.3 all-reduce.1
where the time goes:
time: 584 us; the launch traced here: 581 us
  local copies, waits for them, and re-layouts  229 us (39%)
  waiting for transfers between devices  167 us (29%)
  blocking collectives  81.7 us (14%)
  matrix products  34 us (6%)
  other arithmetic  29.6 us (5%)
  starting transfers between devices  25.2 us (4%)
  between operations  14.9 us (3%)
    gather x2, local copies, waits for them, and re-layouts, code_statistics(): codebook[jnp.arange(subspaces)[None, :], pq_codes]  184 us
    psum x1, waiting for transfers between devices, body(): sums_all, counts_all = lax.psum((sums, counts), ('list', 'rep'))  159 us
    psum x1, blocking collectives, body(): sums_all, counts_all = lax.psum((sums, counts), ('list', 'rep'))  81.7 us
    dot_general x16, matrix products, per_subspace(): lax.dot_general(onehot, part_rows, (((0,), (0,)), ((), ())), preferred_el...  34 us
    convert_element_type x2, local copies, waits for them, and re-layouts, body(): centroids[jnp.clip(got_slot, 0, list_count - 1)].astype(jnp.float32)  12.2 us
  transfers between devices with their start and end apart: 5, of which 3 were waited for; matrix products, arithmetic and copies ran while one was open for 39% of the time, Pallas kernels for 0%

commit v1 on v0

v1 whole, which is shorter than its diff:
```python
import functools

import jax
import jax.numpy as jnp
from jax import lax
from jax.experimental import pallas as pl
from jax.experimental.pallas import tpu as pltpu
from jax.sharding import PartitionSpec as P

prior_weight = 4.0

D = 1024
M = 16
K = 256
DS = 64
ROWS = 256
LISTS = 2048
CAP = 32
NL = 32
NZ = 8
SLOTS = NL * CAP
CW = 128
STEPS = D // CW

F32 = jnp.float32
BF16 = jnp.bfloat16
MESH = pl.DeviceIdType.MESH


def iota(shape, axis):
    return lax.broadcasted_iota(jnp.int32, shape, axis)


def dot(a, b, ca, cb):
    return lax.dot_general(a, b, (((ca,), (cb,)), ((), ())), preferred_element_type=F32)


def onehot(mask):
    return jnp.where(mask, 1.0, 0.0).astype(BF16)


def kernel(
    valid,
    owner,
    slot,
    codes,
    rows_hbm,
    cent_hbm,
    cb_hbm,
    newcb,
    err_out,
    rows,
    cents,
    cb,
    cbd,
    place,
    pos_ref,
    mt_send,
    mt_recv,
    meta,
    pick,
    send,
    recv,
    cent,
    recon,
    ohc,
    err,
    ring_in,
    ring_out,
    cz_send,
    cz_recv,
    cx_send,
    cx_recv,
    rs_send,
    rs_recv,
    ag_send,
    ag_recv,
    et_send,
    et_recv,
    local_sem,
    meta_sem,
    data_ss,
    data_rs,
    ring_ss,
    ring_rs,
    cz_sem,
    cx_sem,
    rs_sem,
    ag_sem,
    et_sem,
):
    me = lax.axis_index("list")
    z = lax.axis_index("rep")

    load_rows = pltpu.make_async_copy(rows_hbm, rows, local_sem.at[0])
    load_cb = pltpu.make_async_copy(cb_hbm, cb, local_sem.at[1])
    load_cents = pltpu.make_async_copy(cent_hbm, cents, local_sem.at[2])
    load_rows.start()
    load_cb.start()
    load_cents.start()

    barrier = pltpu.get_barrier_semaphore()

    def greet(k, c):
        pl.semaphore_signal(
            barrier, inc=1, device_id=(lax.rem(me + k, NL), z), device_id_type=MESH
        )
        return c

    def greet_z(k, c):
        pl.semaphore_signal(
            barrier, inc=1, device_id=(me, lax.rem(z + k, NZ)), device_id_type=MESH
        )
        return c

    lax.fori_loop(1, NL, greet, 0)
    lax.fori_loop(1, NZ, greet_z, 0)

    def peer(k):
        return lax.rem(me + k, NL)

    def copy_to(src, dst, ssem, rsem, who, plane):
        return pltpu.make_async_remote_copy(
            src_ref=src,
            dst_ref=dst,
            send_sem=ssem,
            recv_sem=rsem,
            device_id=(who, plane),
            device_id_type=MESH,
        )

    def pair_at(s):
        return lax.rem(z + (NZ - 1) - s, NZ)

    def column(s):
        return pl.multiple_of(pair_at(s) * CW, CW)

    live = iota((1, ROWS), 1) < valid[0]
    own = jnp.where(live, owner[...], NL)
    named = iota((NL, ROWS), 0) == own
    named_f = jnp.where(named, 1.0, 0.0)
    earlier = onehot(iota((ROWS, ROWS), 0) < iota((ROWS, ROWS), 1))
    before = dot(named_f.astype(BF16), earlier, 1, 0)
    rank = jnp.sum(before * named_f, axis=0, keepdims=True)
    pos = jnp.where(live, own.astype(F32) * CAP + rank, -1.0)
    pos_ref[...] = pos

    def quarter(q):
        i = iota((ROWS, ROWS), 0)
        return ((i // 8) * CAP + q * 8 + i % 8).astype(F32)

    codes_f = jnp.where(live, (codes[...] + 1).astype(F32), 0.0)
    low = (slot[...] % 256).astype(F32)
    high = (slot[...] // 256 + 1).astype(F32)
    which = iota((16, ROWS), 0)
    tail = jnp.where(which == 0, low, jnp.where(which == 1, high, 0.0))
    tail = jnp.where(live, tail, 0.0)
    meta_t = jnp.concatenate([codes_f, tail], axis=0).astype(BF16)
    blank = jnp.zeros((32, ROWS), BF16)
    packed = jnp.zeros((ROWS, 128), F32)
    for q in range(4):
        shifted = jnp.concatenate([meta_t if i == q else blank for i in range(4)], axis=0)
        packed += dot(onehot(quarter(q) == pos), shifted, 1, 1)
    mt_send[...] = packed
    for b in range(4):
        place[pl.ds(b * 256, 256), :] = onehot((iota((256, ROWS), 0) + b * 256).astype(F32) == pos)

    ring_in[0] = jnp.zeros((2, DS, K), F32)
    err[...] = jnp.zeros((SLOTS, CW), F32)

    pl.semaphore_wait(barrier, NL - 1 + NZ - 1)

    def tile8(j):
        return pl.ds(pl.multiple_of(j * 8, 8), 8)

    def tile32(j):
        return pl.ds(pl.multiple_of(j * CAP, CAP), CAP)

    def send_meta(k, c):
        j = peer(k)
        copy_to(mt_send.at[tile8(j)], mt_recv.at[tile8(me)], meta_sem.at[0], meta_sem.at[1], j, z).start()
        return c

    lax.fori_loop(1, NL, send_meta, 0)
    mt_recv[tile8(me), :] = mt_send[tile8(me), :]

    load_rows.wait()

    def bucket_and_send(first):
        both = jnp.concatenate(
            [rows[:, pl.ds(column(first), CW)], rows[:, pl.ds(column(first + 1), CW)]], axis=1
        )
        for b in range(4):
            part = dot(place[pl.ds(b * 256, 256), :], both, 1, 0).astype(BF16)
            send[first, pl.ds(b * 256, 256), :] = part[:, :CW]
            send[first + 1, pl.ds(b * 256, 256), :] = part[:, CW:]
        for h in range(2):
            c = first + h
            for k in range(1, NL):
                j = peer(k)
                copy_to(
                    send.at[c, tile32(j)], recv.at[c, tile32(me)], data_ss.at[c], data_rs.at[c], j, z
                ).start()
            recv[c, tile32(me), :] = send[c, tile32(me), :]

    bucket_and_send(0)

    eye = onehot(iota((ROWS, ROWS), 0) == iota((ROWS, ROWS), 1))
    natural = dot(eye, meta_t, 1, 1)
    code_lane = (iota((ROWS, K), 1) + 1).astype(F32)
    ones = jnp.ones((16, ROWS), BF16)
    for m in range(M):
        tally = dot(ones, onehot(natural[:, m : m + 1] == code_lane), 1, 0)
        for h in range(2):
            cz_send[m // 2, (m % 2) * 2 + h] = tally[0:1, h * 128 : (h + 1) * 128]

    def send_cz(k, c):
        other = lax.rem(z + k, NZ)
        copy_to(cz_send.at[other], cz_recv.at[z], cz_sem.at[0], cz_sem.at[1], me, other).start()
        return c

    lax.fori_loop(1, NZ, send_cz, 0)
    cz_recv[z] = cz_send[z]

    bucket_and_send(2)

    load_cb.wait()
    for p in range(STEPS):
        none = jnp.zeros((DS, K), F32)
        top = jnp.concatenate([cb[2 * p], none], axis=1)
        bottom = jnp.concatenate([none, cb[2 * p + 1]], axis=1)
        block = jnp.concatenate([top, bottom], axis=0)
        coarse = block.astype(BF16)
        cbd[p, 0:CW, :] = coarse
        cbd[p, CW : 2 * CW, :] = (block - coarse.astype(F32)).astype(BF16)

    copy_to(
        cz_send.at[pl.ds(0, NZ - 1)], cz_recv.at[pl.ds(0, NZ - 1)], cz_sem.at[0], cz_sem.at[1], me, z
    ).wait_recv()
    cx_send[...] = jnp.sum(cz_recv[...], axis=0)

    def send_cx(k, c):
        j = peer(k)
        piece = (j // 16) * 2 + lax.rem(j, 2)
        copy_to(cx_send.at[piece], cx_recv.at[me], cx_sem.at[0], cx_sem.at[1], j, z).start()
        return c

    lax.fori_loop(1, NL, send_cx, 0)
    cx_recv[me] = cx_send[(me // 16) * 2 + lax.rem(me, 2)]

    copy_to(
        mt_send.at[pl.ds(0, 248)], mt_recv.at[pl.ds(0, 248)], meta_sem.at[0], meta_sem.at[1], me, z
    ).wait_recv()
    got = mt_recv[...]
    for q in range(4):
        turned = got if q == 0 else pltpu.roll(got, 128 - 32 * q, 1)
        meta[:, q] = turned.reshape(NL, 8, 128)

    def meta_rows(b):
        return meta[pl.ds(b * 8, 8)].reshape(256, 128)

    def build_pick(b, c):
        m = meta_rows(b)
        wanted = m[:, 17:18] * 256.0 + m[:, 16:17] - 256.0
        for t in range(4):
            lanes = (iota((256, 512), 1) + t * 512).astype(F32)
            pick[pl.ds(b * 256, 256), t * 512 : (t + 1) * 512] = onehot(wanted == lanes)
        return c

    lax.fori_loop(0, 4, build_pick, 0)
    load_cents.wait()

    def two_steps(u, carry):
        @pl.when(u < 2)
        def _():
            bucket_and_send(2 * u + 4)

        table = jnp.concatenate(
            [cents[:, pl.ds(column(2 * u), CW)], cents[:, pl.ds(column(2 * u + 1), CW)]], axis=1
        )

        def ahead(b, c):
            r = pl.ds(b * 256, 256)
            centre = dot(pick[r, :], table, 1, 0)
            m = meta_rows(b)
            for h in range(2):
                p = pair_at(2 * u + h)
                cent[h, r, :] = centre[:, h * CW : (h + 1) * CW]
                turned = pltpu.roll(m, lax.rem(128 - 2 * p, 128), 1)
                hot = jnp.concatenate(
                    [onehot(turned[:, 0:1] == code_lane), onehot(turned[:, 1:2] == code_lane)], axis=1
                )
                ohc[h, r, :] = hot
                value = dot(hot, cbd[p], 1, 1)
                recon[h, r, :] = value[:, :CW] + value[:, CW:]
            return c

        lax.fori_loop(0, 4, ahead, 0)

        for h in range(2):
            s = 2 * u + h
            copy_to(
                send.at[s, pl.ds(0, SLOTS - CAP)],
                recv.at[s, pl.ds(0, SLOTS - CAP)],
                data_ss.at[s],
                data_rs.at[s],
                me,
                z,
            ).wait_recv()

            total = jnp.zeros((CW, 2 * K), F32)
            for b in range(4):
                r = pl.ds(b * 256, 256)
                residual = recv[s, r, :].astype(F32) - cent[h, r, :]
                gap = residual - recon[h, r, :]
                err[r, :] += gap * gap
                total += dot(residual.astype(BF16), ohc[h, r, :], 0, 0)
            for a in range(2):
                mine = total[a * DS : (a + 1) * DS, a * K : (a + 1) * K]
                hop = copy_to(
                    ring_out.at[s, a],
                    ring_in.at[lax.rem(s + 1, STEPS), a],
                    ring_ss.at[s, a],
                    ring_rs.at[lax.rem(s + 1, STEPS), a],
                    me,
                    lax.rem(z + 1, NZ),
                )
                arrived = copy_to(
                    ring_out.at[s, a], ring_in.at[s, a], ring_ss.at[s, a], ring_rs.at[s, a], me, z
                )
                if h == 0:
                    pl.when(u > 0)(arrived.wait_recv)
                else:
                    arrived.wait_recv()
                ring_out[s, a] = mine + ring_in[s, a]
                if h == 0:
                    hop.start()
                else:
                    pl.when(u < 3)(hop.start)
        return carry

    lax.fori_loop(0, STEPS // 2, two_steps, 0)

    for a in range(2):
        for d in range(8):
            for h in range(2):
                rs_send[a * 16 + d * 2 + h] = ring_out[
                    STEPS - 1, a, d * 8 : (d + 1) * 8, h * 128 : (h + 1) * 128
                ]

    def send_rs(k, c):
        j = peer(k)
        copy_to(rs_send.at[j], rs_recv.at[me], rs_sem.at[0], rs_sem.at[1], j, z).start()
        return c

    lax.fori_loop(1, NL, send_rs, 0)
    rs_recv[me] = rs_send[me]

    summed = (jnp.sum(err[...], axis=1, keepdims=True) * (1.0 / D)).reshape(NL, 4, 8, 1)
    group = iota((NL, 8, 128), 2) // 32
    tiles = jnp.zeros((NL, 8, 128), F32)
    for q in range(4):
        tiles = jnp.where(group == q, summed[:, q], tiles)
    et_send[...] = tiles.reshape(NL * 8, 128)

    def send_et(k, c):
        j = peer(k)
        copy_to(et_send.at[tile8(j)], et_recv.at[tile8(me)], et_sem.at[0], et_sem.at[1], j, z).start()
        return c

    lax.fori_loop(1, NL, send_et, 0)
    et_recv[tile8(me), :] = et_send[tile8(me), :]

    def wait_all(src, dst, sem):
        whole = copy_to(src, dst, sem.at[0], sem.at[1], me, z)
        return whole

    first31 = pl.ds(0, NL - 1)
    cx_all = wait_all(cx_recv.at[first31], cx_recv.at[first31], cx_sem)
    rs_all = wait_all(rs_send.at[first31], rs_recv.at[first31], rs_sem)
    ag_all = wait_all(ag_recv.at[first31], ag_recv.at[first31], ag_sem)
    et_all = wait_all(et_send.at[pl.ds(0, 248)], et_recv.at[pl.ds(0, 248)], et_sem)

    cx_all.wait_recv()
    count = jnp.sum(cx_recv[...], axis=0)
    rs_all.wait_recv()
    total = jnp.sum(rs_recv[...], axis=0)
    old = cb[
        2 * z + me // 16,
        pl.ds(pl.multiple_of(lax.rem(me // 2, 8) * 8, 8), 8),
        pl.ds(pl.multiple_of(lax.rem(me, 2) * 128, 128), 128),
    ]
    ag_send[...] = (total + prior_weight * old) / (count + prior_weight)

    def send_ag(k, c):
        j = peer(k)
        copy_to(ag_send, ag_recv.at[me], ag_sem.at[0], ag_sem.at[1], j, z).start()
        return c

    lax.fori_loop(1, NL, send_ag, 0)
    ag_recv[me] = ag_send[...]

    et_all.wait_recv()
    final = jnp.zeros((1, ROWS), F32)
    where = pos_ref[...]
    for q in range(4):
        e = et_recv[:, q * 32 : q * 32 + 1]
        final += jnp.sum(jnp.where(quarter(q) == where, e, 0.0), axis=0, keepdims=True)
    err_out[...] = final

    ag_all.wait_recv()
    for a in range(2):
        for d in range(8):
            for h in range(2):
                newcb[a, d * 8 : (d + 1) * 8, h * 128 : (h + 1) * 128] = ag_recv[a * 16 + d * 2 + h]

    copy_to(
        mt_send.at[pl.ds(0, 248)], mt_recv.at[pl.ds(0, 248)], meta_sem.at[0], meta_sem.at[1], me, z
    ).wait_send()
    copy_to(
        cz_send.at[pl.ds(0, NZ - 1)], cz_recv.at[pl.ds(0, NZ - 1)], cz_sem.at[0], cz_sem.at[1], me, z
    ).wait_send()

    def drain(s, c):
        copy_to(
            send.at[s, pl.ds(0, SLOTS - CAP)],
            recv.at[s, pl.ds(0, SLOTS - CAP)],
            data_ss.at[s],
            data_rs.at[s],
            me,
            z,
        ).wait_send()
        return c

    lax.fori_loop(0, STEPS, drain, 0)

    def drain_ring(s, c):
        for a in range(2):
            copy_to(
                ring_out.at[s, a], ring_in.at[s, a], ring_ss.at[s, a], ring_rs.at[s, a], me, z
            ).wait_send()
        return c

    lax.fori_loop(0, STEPS - 1, drain_ring, 0)
    cx_all.wait_send()
    rs_all.wait_send()
    et_all.wait_send()
    ag_all.wait_send()


def body(memory_rows, list_owner, list_slot, pq_codes, valid_rows, centroids, codebook):
    vmem = pl.BlockSpec(memory_space=pltpu.VMEM)
    anywhere = pl.BlockSpec(memory_space=pl.ANY)
    dma = pltpu.SemaphoreType.DMA
    newcb, err = pl.pallas_call(
        kernel,
        out_shape=(
            jax.ShapeDtypeStruct((2, DS, K), F32),
            jax.ShapeDtypeStruct((1, ROWS), F32),
        ),
        in_specs=[pl.BlockSpec(memory_space=pltpu.SMEM), vmem, vmem, vmem, anywhere, anywhere, anywhere],
        out_specs=(vmem, vmem),
        scratch_shapes=[
            pltpu.VMEM((ROWS, D), BF16),
            pltpu.VMEM((LISTS, D), BF16),
            pltpu.VMEM((M, DS, K), F32),
            pltpu.VMEM((STEPS, 2 * CW, 2 * K), BF16),
            pltpu.VMEM((SLOTS, ROWS), BF16),
            pltpu.VMEM((1, ROWS), F32),
            pltpu.VMEM((NL * 8, 128), F32),
            pltpu.VMEM((NL * 8, 128), F32),
            pltpu.VMEM((NL, 4, 8, 128), F32),
            pltpu.VMEM((SLOTS, LISTS), BF16),
            pltpu.VMEM((STEPS, SLOTS, CW), BF16),
            pltpu.VMEM((STEPS, SLOTS, CW), BF16),
            pltpu.VMEM((2, SLOTS, CW), F32),
            pltpu.VMEM((2, SLOTS, CW), F32),
            pltpu.VMEM((2, SLOTS, 2 * K), BF16),
            pltpu.VMEM((SLOTS, CW), F32),
            pltpu.VMEM((STEPS, 2, DS, K), F32),
            pltpu.VMEM((STEPS, 2, DS, K), F32),
            pltpu.VMEM((NZ, 4, 1, 128), F32),
            pltpu.VMEM((NZ, 4, 1, 128), F32),
            pltpu.VMEM((4, 1, 128), F32),
            pltpu.VMEM((NL, 1, 128), F32),
            pltpu.VMEM((NL, 8, 128), F32),
            pltpu.VMEM((NL, 8, 128), F32),
            pltpu.VMEM((8, 128), F32),
            pltpu.VMEM((NL, 8, 128), F32),
            pltpu.VMEM((NL * 8, 128), F32),
            pltpu.VMEM((NL * 8, 128), F32),
            dma((3,)),
            dma((2,)),
            dma((STEPS,)),
            dma((STEPS,)),
            dma((STEPS, 2)),
            dma((STEPS, 2)),
            dma((2,)),
            dma((2,)),
            dma((2,)),
            dma((2,)),
            dma((2,)),
        ],
        compiler_params=pltpu.CompilerParams(
            collective_id=0, has_side_effects=True, vmem_limit_bytes=56 * 2**20
        ),
    )(
        valid_rows,
        list_owner.T,
        list_slot.reshape(1, -1),
        pq_codes.T,
        memory_rows,
        centroids,
        codebook.transpose(0, 2, 1),
    )
    return newcb.transpose(0, 2, 1), err.reshape(-1)


def solution(mesh):
    in_specs = (
        P(("list", "rep"), None),
        P(("list", "rep"), None),
        P(("list", "rep")),
        P(("list", "rep"), None),
        P(("list", "rep")),
        P("list", None),
        P(),
    )
    out_specs = (P("rep", None, None), P(("list", "rep")))
    return jax.shard_map(body, mesh=mesh, in_specs=in_specs, out_specs=out_specs, check_vma=False)
```

time: 584 us -> 69.1 us (0.12)
  local copies, waits for them, and re-layouts: 229 us -> 2.8 us
  waiting for transfers between devices: 167 us -> 0 us
  blocking collectives: 81.7 us -> 0 us
  Pallas kernels: 0 us -> 64.8 us
  matrix products: 34 us -> 0 us
  other arithmetic: 29.6 us -> 0 us
  starting transfers between devices: 25.2 us -> 0 us
  between operations: 14.9 us -> 1.29 us
    gather x4 -> x0, local copies, waits for them, and re-layouts: 194 us -> none  [the longest x2 184 us: code_statistics(): codebook[jnp.arange(subspaces)[None, :], pq_codes]]
    psum x1 -> x0, waiting for transfers between devices: 159 us -> none  [body(): sums_all, counts_all = lax.psum((sums, counts), ('list', 'rep'))]
    psum x1 -> x0, blocking collectives: 81.7 us -> none  [body(): sums_all, counts_all = lax.psum((sums, counts), ('list', 'rep'))]
    pallas_call x0 -> x1, Pallas kernels: none -> 64.8 us  [body(): pl.pallas_call(kernel, out_shape=(jax.ShapeDtypeStruct((2, DS, K), F32),...]
    dot_general x16 -> x0, matrix products: 34 us -> none  [per_subspace(): lax.dot_general(onehot, part_rows, (((0,), (0,)), ((), ())), preferred_el...]
    all_to_all x4 -> x0, starting transfers between devices: 25 us -> none  [the longest x1 8.59 us: body(): lax.all_to_all(send_slot.reshape(owners, capacity), 'list', split_axis=0,...]
    convert_element_type x3 -> x0, local copies, waits for them, and re-layouts: 19.1 us -> none  [the longest x2 12.2 us: body(): centroids[jnp.clip(got_slot, 0, list_count - 1)].astype(jnp.float32)]
    reduce_sum x18 -> x0, other arithmetic: 11.5 us -> none  [the longest x16 5.59 us: per_subspace(): counts_one = jnp.sum(onehot.astype(jnp.float32), axis=0)]
  transfers between devices with their start and end apart: 5 -> 0, of which waited for: 3 -> 0; matrix products, arithmetic and copies ran while one was open for 39% -> 0% of each run, Pallas kernels for 0% -> 0%
where the time goes in v1:
time: 69.1 us; the launch traced here: 68.9 us
  Pallas kernels  64.8 us (94%)
  local copies, waits for them, and re-layouts  2.8 us (4%)
  between operations  1.29 us (2%)
    pallas_call x1, Pallas kernels, body(): pl.pallas_call(kernel, out_shape=(jax.ShapeDtypeStruct((2, DS, K), F32),...  64.8 us
    unnamed x2, local copies, waits for them, and re-layouts  2.8 us

profile of v1, /device:TPU:1, one launch (start us, length us, event | category | flops | bytes accessed | tf_op | source)
XLA Modules:
  0.0 68.9 jit_solution(14751920672107908890)
XLA Ops:
  1.3 64.8 %shard_map.86 = (f32[2,64,256]{2,1,0:T(8,128)}, f32[1,256]{1,0:T(1,128)}) custom-call(s32[1]{0:T(128)S(6)} %copy.11.valid, s32[1,256]{1,0:T(1,128)} %bitcast.10, s32[1,256]{1,0:T(1,128)} %bitcast.11, s32[16,256]{1,0:T(8,128)} %bitcast.8, bf16[256,1024]{1,0:T(8,128)(2,1)} %rows_hbm.1, bf16[2048,1024]{1,0:T(8,128)(2,1)} %cent_hbm.1, f32[16,64,256]{2,1,0:T(8,128)} %bitcast.6), custom_call_target="tpu_custom_call" | custom-call | tf_op jit(solution)/shard_map/pallas_call | solution.py:455
  66.1 1.6 %copy.12 = f32[2,256,64]{1,2,0:T(8,128)} copy(f32[2,256,64]{1,2,0:T(8,128)} %bitcast.7) | data formatting | bytes 262144
  67.7 1.2 %copy.13 = f32[256]{0:T(256)} copy(f32[256]{0:T(256)} %bitcast.9) | data formatting | bytes 2048

commit v2 on v1

--- a/solution.py
+++ b/solution.py
@@ -65,12 +65,17 @@
     recon,
     ohc,
     err,
-    ring_in,
-    ring_out,
+    zin,
+    zout,
+    sib_send,
+    sib_recv,
+    held,
     cz_send,
     cz_recv,
     cx_send,
     cx_recv,
+    hand_send,
+    hand_recv,
     rs_send,
     rs_recv,
     ag_send,
@@ -81,10 +86,12 @@
     meta_sem,
     data_ss,
     data_rs,
-    ring_ss,
-    ring_rs,
+    z_sem,
+    sib_ss,
+    sib_rs,
     cz_sem,
     cx_sem,
+    hand_sem,
     rs_sem,
     ag_sem,
     et_sem,
@@ -113,8 +120,19 @@
         )
         return c
 
+    def greet_planes(k, c):
+        for step in (1, NZ - 1):
+            pl.semaphore_signal(
+                barrier,
+                inc=1,
+                device_id=(lax.rem(me + k, NL), lax.rem(z + step, NZ)),
+                device_id_type=MESH,
+            )
+        return c
+
     lax.fori_loop(1, NL, greet, 0)
     lax.fori_loop(1, NZ, greet_z, 0)
+    lax.fori_loop(1, NL, greet_planes, 0)
 
     def peer(k):
         return lax.rem(me + k, NL)
@@ -129,11 +147,11 @@
             device_id_type=MESH,
         )
 
-    def pair_at(s):
-        return lax.rem(z + (NZ - 1) - s, NZ)
-
-    def column(s):
-        return pl.multiple_of(pair_at(s) * CW, CW)
+    def pair_at(u, h):
+        return lax.rem(z + (3 - u if h else 4 + u), NZ)
+
+    def column(u, h):
+        return pl.multiple_of(pair_at(u, h) * CW, CW)
 
     live = iota((1, ROWS), 1) < valid[0]
     own = jnp.where(live, owner[...], NL)
@@ -165,49 +183,54 @@
     for b in range(4):
         place[pl.ds(b * 256, 256), :] = onehot((iota((256, ROWS), 0) + b * 256).astype(F32) == pos)
 
-    ring_in[0] = jnp.zeros((2, DS, K), F32)
     err[...] = jnp.zeros((SLOTS, CW), F32)
 
-    pl.semaphore_wait(barrier, NL - 1 + NZ - 1)
-
-    def tile8(j):
-        return pl.ds(pl.multiple_of(j * 8, 8), 8)
-
-    def tile32(j):
-        return pl.ds(pl.multiple_of(j * CAP, CAP), CAP)
-
-    def send_meta(k, c):
-        j = peer(k)
-        copy_to(mt_send.at[tile8(j)], mt_recv.at[tile8(me)], meta_sem.at[0], meta_sem.at[1], j, z).start()
-        return c
-
-    lax.fori_loop(1, NL, send_meta, 0)
-    mt_recv[tile8(me), :] = mt_send[tile8(me), :]
-
     load_rows.wait()
 
-    def bucket_and_send(first):
+    def bucket(v):
+        first = 2 * v
         both = jnp.concatenate(
-            [rows[:, pl.ds(column(first), CW)], rows[:, pl.ds(column(first + 1), CW)]], axis=1
+            [rows[:, pl.ds(column(v, 0), CW)], rows[:, pl.ds(column(v, 1), CW)]], axis=1
         )
         for b in range(4):
             part = dot(place[pl.ds(b * 256, 256), :], both, 1, 0).astype(BF16)
             send[first, pl.ds(b * 256, 256), :] = part[:, :CW]
             send[first + 1, pl.ds(b * 256, 256), :] = part[:, CW:]
-        for h in range(2):
-            c = first + h
-            for k in range(1, NL):
-                j = peer(k)
-                copy_to(
-                    send.at[c, tile32(j)], recv.at[c, tile32(me)], data_ss.at[c], data_rs.at[c], j, z
-                ).start()
-            recv[c, tile32(me), :] = send[c, tile32(me), :]
-
-    bucket_and_send(0)
+
+    bucket(0)
+    pl.semaphore_wait(barrier, 3 * (NL - 1) + NZ - 1)
+
+    def tile8(j):
+        return pl.ds(pl.multiple_of(j * 8, 8), 8)
+
+    def tile32(j):
+        return pl.ds(pl.multiple_of(j * CAP, CAP), CAP)
+
+    def start(v, h):
+        c = 2 * v + h
+        for k in range(1, NL):
+            j = peer(k)
+            copy_to(
+                send.at[c, tile32(j)], recv.at[c, tile32(me)], data_ss.at[c], data_rs.at[c], j, z
+            ).start()
+        recv[c, tile32(me), :] = send[c, tile32(me), :]
+
+    def send_meta(k, c):
+        j = peer(k)
+        copy_to(mt_send.at[tile8(j)], mt_recv.at[tile8(me)], meta_sem.at[0], meta_sem.at[1], j, z).start()
+        return c
+
+    lax.fori_loop(1, NL, send_meta, 0)
+    mt_recv[tile8(me), :] = mt_send[tile8(me), :]
+
+
+    start(0, 0)
+    start(0, 1)
 
     eye = onehot(iota((ROWS, ROWS), 0) == iota((ROWS, ROWS), 1))
     natural = dot(eye, meta_t, 1, 1)
     code_lane = (iota((ROWS, K), 1) + 1).astype(F32)
+    code_lane2 = (iota((1024, K), 1) + 1).astype(F32)
     ones = jnp.ones((16, ROWS), BF16)
     for m in range(M):
         tally = dot(ones, onehot(natural[:, m : m + 1] == code_lane), 1, 0)
@@ -221,8 +244,6 @@
 
     lax.fori_loop(1, NZ, send_cz, 0)
     cz_recv[z] = cz_send[z]
-
-    bucket_and_send(2)
 
     load_cb.wait()
     for p in range(STEPS):
@@ -235,20 +256,6 @@
         cbd[p, CW : 2 * CW, :] = (block - coarse.astype(F32)).astype(BF16)
 
     copy_to(
-        cz_send.at[pl.ds(0, NZ - 1)], cz_recv.at[pl.ds(0, NZ - 1)], cz_sem.at[0], cz_sem.at[1], me, z
-    ).wait_recv()
-    cx_send[...] = jnp.sum(cz_recv[...], axis=0)
-
-    def send_cx(k, c):
-        j = peer(k)
-        piece = (j // 16) * 2 + lax.rem(j, 2)
-        copy_to(cx_send.at[piece], cx_recv.at[me], cx_sem.at[0], cx_sem.at[1], j, z).start()
-        return c
-
-    lax.fori_loop(1, NL, send_cx, 0)
-    cx_recv[me] = cx_send[(me // 16) * 2 + lax.rem(me, 2)]
-
-    copy_to(
         mt_send.at[pl.ds(0, 248)], mt_recv.at[pl.ds(0, 248)], meta_sem.at[0], meta_sem.at[1], me, z
     ).wait_recv()
     got = mt_recv[...]
@@ -257,45 +264,93 @@
         meta[:, q] = turned.reshape(NL, 8, 128)
 
     def meta_rows(b):
-        return meta[pl.ds(b * 8, 8)].reshape(256, 128)
+        return meta[pl.ds(b * 32, 32)].reshape(1024, 128)
 
     def build_pick(b, c):
         m = meta_rows(b)
         wanted = m[:, 17:18] * 256.0 + m[:, 16:17] - 256.0
         for t in range(4):
-            lanes = (iota((256, 512), 1) + t * 512).astype(F32)
-            pick[pl.ds(b * 256, 256), t * 512 : (t + 1) * 512] = onehot(wanted == lanes)
-        return c
-
-    lax.fori_loop(0, 4, build_pick, 0)
+            lanes = (iota((1024, 512), 1) + t * 512).astype(F32)
+            pick[pl.ds(b * 1024, 1024), t * 512 : (t + 1) * 512] = onehot(wanted == lanes)
+        return c
+
+    lax.fori_loop(0, 1, build_pick, 0)
     load_cents.wait()
 
+    core = lax.rem(me, 2)
+    sibling = me + 1 - 2 * core
+
+    def share(s, mine, theirs):
+        zout[s] = mine
+        sib_send[s] = theirs
+        copy_to(sib_send.at[s], sib_recv.at[s], sib_ss.at[s], sib_rs.at[s], sibling, z).start()
+
+    def forward(u, h):
+        s = 2 * u + h
+        copy_to(sib_send.at[s], sib_recv.at[s], sib_ss.at[s], sib_rs.at[s], sibling, z).wait_recv()
+        zout[s] = zout[s] + sib_recv[s]
+        copy_to(zout.at[s], zin.at[s], z_sem.at[0], z_sem.at[1], me, pair_at(u, h)).start()
+
+    def pass_counts():
+        copy_to(
+            cz_send.at[pl.ds(0, NZ - 1)], cz_recv.at[pl.ds(0, NZ - 1)], cz_sem.at[0], cz_sem.at[1], me, z
+        ).wait_recv()
+        cx_send[...] = jnp.sum(cz_recv[...], axis=0)
+
+        def send_cx(k, c):
+            j = peer(k)
+            piece = (j // 16) * 2 + lax.rem(j, 2)
+            copy_to(cx_send.at[piece], cx_recv.at[me], cx_sem.at[0], cx_sem.at[1], j, z).start()
+            return c
+
+        lax.fori_loop(1, NL, send_cx, 0)
+        cx_recv[me] = cx_send[(me // 16) * 2 + lax.rem(me, 2)]
+
+    def piece_of(sums, i):
+        a, d, h = i // 16, (i // 2) % 8, i % 2
+        return sums[a][d * 8 : (d + 1) * 8, h * 128 : (h + 1) * 128]
+
+    def send_hand(k, c):
+        j = peer(k)
+        copy_to(
+            hand_send.at[j], hand_recv.at[me], hand_sem.at[0], hand_sem.at[1], j, pair_at(3, 0)
+        ).start()
+        return c
+
     def two_steps(u, carry):
-        @pl.when(u < 2)
+        @pl.when(u < 3)
         def _():
-            bucket_and_send(2 * u + 4)
+            bucket(u + 1)
+            start(u + 1, 0)
 
         table = jnp.concatenate(
-            [cents[:, pl.ds(column(2 * u), CW)], cents[:, pl.ds(column(2 * u + 1), CW)]], axis=1
+            [cents[:, pl.ds(column(u, 0), CW)], cents[:, pl.ds(column(u, 1), CW)]], axis=1
         )
 
         def ahead(b, c):
-            r = pl.ds(b * 256, 256)
+            r = pl.ds(b * 1024, 1024)
             centre = dot(pick[r, :], table, 1, 0)
             m = meta_rows(b)
             for h in range(2):
-                p = pair_at(2 * u + h)
+                p = pair_at(u, h)
                 cent[h, r, :] = centre[:, h * CW : (h + 1) * CW]
                 turned = pltpu.roll(m, lax.rem(128 - 2 * p, 128), 1)
                 hot = jnp.concatenate(
-                    [onehot(turned[:, 0:1] == code_lane), onehot(turned[:, 1:2] == code_lane)], axis=1
+                    [onehot(turned[:, 0:1] == code_lane2), onehot(turned[:, 1:2] == code_lane2)], axis=1
                 )
                 ohc[h, r, :] = hot
                 value = dot(hot, cbd[p], 1, 1)
                 recon[h, r, :] = value[:, :CW] + value[:, CW:]
             return c
 
-        lax.fori_loop(0, 4, ahead, 0)
+        lax.fori_loop(0, 1, ahead, 0)
+
+        @pl.when(u > 0)
+        def _():
+            forward(u - 1, 0)
+            forward(u - 1, 1)
+
+        pl.when(u == 1)(pass_counts)
 
         for h in range(2):
             s = 2 * u + h
@@ -315,38 +370,39 @@
                 gap = residual - recon[h, r, :]
                 err[r, :] += gap * gap
                 total += dot(residual.astype(BF16), ohc[h, r, :], 0, 0)
-            for a in range(2):
-                mine = total[a * DS : (a + 1) * DS, a * K : (a + 1) * K]
-                hop = copy_to(
-                    ring_out.at[s, a],
-                    ring_in.at[lax.rem(s + 1, STEPS), a],
-                    ring_ss.at[s, a],
-                    ring_rs.at[lax.rem(s + 1, STEPS), a],
-                    me,
-                    lax.rem(z + 1, NZ),
-                )
-                arrived = copy_to(
-                    ring_out.at[s, a], ring_in.at[s, a], ring_ss.at[s, a], ring_rs.at[s, a], me, z
-                )
+            first, second = total[:DS, :K], total[DS:, K:]
+            mine = jnp.where(core == 0, first, second)
+            theirs = jnp.where(core == 0, second, first)
+
+            @pl.when(u < 3)
+            def _():
+                share(s, mine, theirs)
                 if h == 0:
-                    pl.when(u > 0)(arrived.wait_recv)
+                    start(u + 1, 1)
+
+            @pl.when(u == 3)
+            def _():
+                if h == 1:
+                    held[0] = first
+                    held[1] = second
                 else:
-                    arrived.wait_recv()
-                ring_out[s, a] = mine + ring_in[s, a]
-                if h == 0:
-                    hop.start()
-                else:
-                    pl.when(u < 3)(hop.start)
+                    for i in range(NL):
+                        hand_send[i] = piece_of((first, second), i)
+                    lax.fori_loop(0, NL, send_hand, 0)
+
         return carry
 
     lax.fori_loop(0, STEPS // 2, two_steps, 0)
 
-    for a in range(2):
-        for d in range(8):
-            for h in range(2):
-                rs_send[a * 16 + d * 2 + h] = ring_out[
-                    STEPS - 1, a, d * 8 : (d + 1) * 8, h * 128 : (h + 1) * 128
-                ]
+    z_all = copy_to(
+        zout, zin, z_sem.at[0], z_sem.at[1], me, z
+    )
+    z_all.wait_recv()
+    others = jnp.sum(zin[...], axis=0)
+    plane_sum = [held[a] + jnp.where(core == a, others, 0.0) for a in range(2)]
+
+    for i in range(NL):
+        rs_send[i] = piece_of(plane_sum, i)
 
     def send_rs(k, c):
         j = peer(k)
@@ -357,19 +413,20 @@
     rs_recv[me] = rs_send[me]
 
     summed = (jnp.sum(err[...], axis=1, keepdims=True) * (1.0 / D)).reshape(NL, 4, 8, 1)
-    group = iota((NL, 8, 128), 2) // 32
+    lane = iota((NL, 8, 128), 2)
     tiles = jnp.zeros((NL, 8, 128), F32)
     for q in range(4):
-        tiles = jnp.where(group == q, summed[:, q], tiles)
-    et_send[...] = tiles.reshape(NL * 8, 128)
+        tiles = jnp.where(lane // 32 == q, summed[:, q], tiles)
+    tiles = jnp.where((lane % 32) // 4 == iota((NL, 8, 128), 1), tiles, 0.0)
+    et_send[...] = jnp.sum(tiles, axis=1, keepdims=True)
 
     def send_et(k, c):
         j = peer(k)
-        copy_to(et_send.at[tile8(j)], et_recv.at[tile8(me)], et_sem.at[0], et_sem.at[1], j, z).start()
+        copy_to(et_send.at[j], et_recv.at[me], et_sem.at[0], et_sem.at[1], j, z).start()
         return c
 
     lax.fori_loop(1, NL, send_et, 0)
-    et_recv[tile8(me), :] = et_send[tile8(me), :]
+    et_recv[me] = et_send[me]
 
     def wait_all(src, dst, sem):
         whole = copy_to(src, dst, sem.at[0], sem.at[1], me, z)
@@ -378,13 +435,15 @@
     first31 = pl.ds(0, NL - 1)
     cx_all = wait_all(cx_recv.at[first31], cx_recv.at[first31], cx_sem)
     rs_all = wait_all(rs_send.at[first31], rs_recv.at[first31], rs_sem)
+    hand_all = wait_all(hand_send, hand_recv, hand_sem)
     ag_all = wait_all(ag_recv.at[first31], ag_recv.at[first31], ag_sem)
-    et_all = wait_all(et_send.at[pl.ds(0, 248)], et_recv.at[pl.ds(0, 248)], et_sem)
+    et_all = wait_all(et_send.at[first31], et_recv.at[first31], et_sem)
 
     cx_all.wait_recv()
     count = jnp.sum(cx_recv[...], axis=0)
     rs_all.wait_recv()
-    total = jnp.sum(rs_recv[...], axis=0)
+    hand_all.wait_recv()
+    total = jnp.sum(rs_recv[...] + hand_recv[...], axis=0)
     old = cb[
         2 * z + me // 16,
         pl.ds(pl.multiple_of(lax.rem(me // 2, 8) * 8, 8), 8),
@@ -401,12 +460,17 @@
     ag_recv[me] = ag_send[...]
 
     et_all.wait_recv()
-    final = jnp.zeros((1, ROWS), F32)
-    where = pos_ref[...]
-    for q in range(4):
-        e = et_recv[:, q * 32 : q * 32 + 1]
-        final += jnp.sum(jnp.where(quarter(q) == where, e, 0.0), axis=0, keepdims=True)
-    err_out[...] = final
+    rest = et_recv[...].reshape(NL, 128)
+    holder = pos_ref[...]
+    owner_of = jnp.floor(holder * (1.0 / CAP))
+    at = onehot(iota((128, ROWS), 0).astype(F32) == (holder - owner_of * CAP) * 4.0)
+    picked = jnp.zeros((NL, ROWS), F32)
+    for _ in range(3):
+        part = rest.astype(BF16)
+        rest = rest - part.astype(F32)
+        picked += dot(part, at, 1, 0)
+    belongs = iota((NL, ROWS), 0).astype(F32) == owner_of
+    err_out[...] = jnp.sum(jnp.where(belongs, picked, 0.0), axis=0, keepdims=True)
 
     ag_all.wait_recv()
     for a in range(2):
@@ -434,18 +498,23 @@
 
     lax.fori_loop(0, STEPS, drain, 0)
 
-    def drain_ring(s, c):
-        for a in range(2):
-            copy_to(
-                ring_out.at[s, a], ring_in.at[s, a], ring_ss.at[s, a], ring_rs.at[s, a], me, z
-            ).wait_send()
-        return c
-
-    lax.fori_loop(0, STEPS - 1, drain_ring, 0)
+    z_all.wait_send()
+
+    def drain_share(i, c):
+        copy_to(sib_send.at[i], sib_recv.at[i], sib_ss.at[i], sib_rs.at[i], sibling, z).wait_send()
+        return c
+
+    lax.fori_loop(0, STEPS - 2, drain_share, 0)
     cx_all.wait_send()
+    hand_all.wait_send()
     rs_all.wait_send()
     et_all.wait_send()
     ag_all.wait_send()
+
+
+def hand_over(newcb_in, err_in, newcb_out, err_out):
+    newcb_out[...] = newcb_in[...]
+    err_out[...] = err_in[...]
 
 
 def body(memory_rows, list_owner, list_slot, pq_codes, valid_rows, centroids, codebook):
@@ -477,24 +546,31 @@
             pltpu.VMEM((2, SLOTS, CW), F32),
             pltpu.VMEM((2, SLOTS, 2 * K), BF16),
             pltpu.VMEM((SLOTS, CW), F32),
-            pltpu.VMEM((STEPS, 2, DS, K), F32),
-            pltpu.VMEM((STEPS, 2, DS, K), F32),
+            pltpu.VMEM((STEPS - 2, DS, K), F32),
+            pltpu.VMEM((STEPS - 2, DS, K), F32),
+            pltpu.VMEM((STEPS - 2, DS, K), F32),
+            pltpu.VMEM((STEPS - 2, DS, K), F32),
+            pltpu.VMEM((2, DS, K), F32),
             pltpu.VMEM((NZ, 4, 1, 128), F32),
             pltpu.VMEM((NZ, 4, 1, 128), F32),
             pltpu.VMEM((4, 1, 128), F32),
             pltpu.VMEM((NL, 1, 128), F32),
             pltpu.VMEM((NL, 8, 128), F32),
             pltpu.VMEM((NL, 8, 128), F32),
+            pltpu.VMEM((NL, 8, 128), F32),
+            pltpu.VMEM((NL, 8, 128), F32),
             pltpu.VMEM((8, 128), F32),
             pltpu.VMEM((NL, 8, 128), F32),
-            pltpu.VMEM((NL * 8, 128), F32),
-            pltpu.VMEM((NL * 8, 128), F32),
+            pltpu.VMEM((NL, 1, 128), F32),
+            pltpu.VMEM((NL, 1, 128), F32),
             dma((3,)),
             dma((2,)),
             dma((STEPS,)),
             dma((STEPS,)),
-            dma((STEPS, 2)),
-            dma((STEPS, 2)),
+            dma((2,)),
+            dma((STEPS - 2,)),
+            dma((STEPS - 2,)),
+            dma((2,)),
             dma((2,)),
             dma((2,)),
             dma((2,)),
@@ -513,6 +589,15 @@
         centroids,
         codebook.transpose(0, 2, 1),
     )
+    newcb, err = pl.pallas_call(
+        hand_over,
+        out_shape=(
+            jax.ShapeDtypeStruct((2, DS, K), F32),
+            jax.ShapeDtypeStruct((1, ROWS), F32),
+        ),
+        in_specs=[vmem, vmem],
+        out_specs=(vmem, vmem),
+    )(newcb, err)
     return newcb.transpose(0, 2, 1), err.reshape(-1)
 
 

time: 69.1 us -> 58.2 us (0.84)
  Pallas kernels: 64.8 us -> 56.7 us
  local copies, waits for them, and re-layouts: 2.8 us -> 0 us
    pallas_call x1, Pallas kernels: 64.8 us -> 55.1 us  [body(): pl.pallas_call(kernel, out_shape=(jax.ShapeDtypeStruct((2, DS, K), F32),...]
    unnamed x2 -> x0, local copies, waits for them, and re-layouts: 2.8 us -> none
    pallas_call x0 -> x1, Pallas kernels: none -> 1.57 us  [body(): pl.pallas_call(hand_over, out_shape=(jax.ShapeDtypeStruct((2, DS, K), F32...]
where the time goes in v2:
time: 58.2 us; the launch traced here: 58 us
  Pallas kernels  56.7 us (97%)
  between operations  1.29 us (2%)
    pallas_call x1, Pallas kernels, body(): pl.pallas_call(kernel, out_shape=(jax.ShapeDtypeStruct((2, DS, K), F32),...  55.1 us
    pallas_call x1, Pallas kernels, body(): pl.pallas_call(hand_over, out_shape=(jax.ShapeDtypeStruct((2, DS, K), F32...  1.57 us

profile of v2, /device:TPU:1, one launch (start us, length us, event | category | flops | bytes accessed | tf_op | source)
XLA Modules:
  0.0 58.0 jit_solution(2515999693930758194)
XLA Ops:
  1.3 55.1 %shard_map.86 = (f32[2,64,256]{2,1,0:T(8,128)}, f32[1,256]{1,0:T(1,128)}) custom-call(s32[1]{0:T(128)S(6)} %copy.9.valid, s32[1,256]{1,0:T(1,128)} %bitcast.8, s32[1,256]{1,0:T(1,128)} %bitcast.9, s32[16,256]{1,0:T(8,128)} %bitcast.7, bf16[256,1024]{1,0:T(8,128)(2,1)} %rows_hbm.1, bf16[2048,1024]{1,0:T(8,128)(2,1)} %cent_hbm.1, f32[16,64,256]{2,1,0:T(8,128)} %bitcast.6), custom_call_target="tpu_custom_call" | custom-call | tf_op jit(solution)/shard_map/pallas_call | solution.py:524
  56.4 1.6 %shard_map.87 = (f32[2,64,256]{2,1,0:T(8,128)}, f32[1,256]{1,0:T(1,128)}) custom-call(f32[2,64,256]{2,1,0:T(8,128)} %get-tuple-element.6.newcb_in, f32[1,256]{1,0:T(1,128)} %get-tuple-element.7.err_in), custom_call_target="tpu_custom_call" | custom-call | tf_op jit(solution)/shard_map/pallas_call | solution.py:592

commit v3 on v2

--- a/solution.py
+++ b/solution.py
@@ -79,7 +79,6 @@
     rs_send,
     rs_recv,
     ag_send,
-    ag_recv,
     et_send,
     et_recv,
     local_sem,
@@ -137,6 +136,18 @@
     def peer(k):
         return lax.rem(me + k, NL)
 
+    def ring(steps):
+        return min(steps, 4 - steps)
+
+    offsets = [(dx, dy, dc) for dx in range(4) for dy in range(4) for dc in range(2)]
+    offsets.sort(key=lambda o: -(ring(o[0]) + ring(o[1])))
+
+    def far_first():
+        x, y, c = me // 8, lax.rem(me // 2, 4), lax.rem(me, 2)
+        for dx, dy, dc in offsets[:-2]:
+            yield (lax.rem(x + dx, 4) * 4 + lax.rem(y + dy, 4)) * 2 + lax.rem(c + dc, 2)
+        yield me + 1 - 2 * c
+
     def copy_to(src, dst, ssem, rsem, who, plane):
         return pltpu.make_async_remote_copy(
             src_ref=src,
@@ -404,12 +415,8 @@
     for i in range(NL):
         rs_send[i] = piece_of(plane_sum, i)
 
-    def send_rs(k, c):
-        j = peer(k)
+    for j in far_first():
         copy_to(rs_send.at[j], rs_recv.at[me], rs_sem.at[0], rs_sem.at[1], j, z).start()
-        return c
-
-    lax.fori_loop(1, NL, send_rs, 0)
     rs_recv[me] = rs_send[me]
 
     summed = (jnp.sum(err[...], axis=1, keepdims=True) * (1.0 / D)).reshape(NL, 4, 8, 1)
@@ -436,7 +443,7 @@
     cx_all = wait_all(cx_recv.at[first31], cx_recv.at[first31], cx_sem)
     rs_all = wait_all(rs_send.at[first31], rs_recv.at[first31], rs_sem)
     hand_all = wait_all(hand_send, hand_recv, hand_sem)
-    ag_all = wait_all(ag_recv.at[first31], ag_recv.at[first31], ag_sem)
+    ag_all = wait_all(rs_send.at[first31], rs_recv.at[first31], ag_sem)
     et_all = wait_all(et_send.at[first31], et_recv.at[first31], et_sem)
 
     cx_all.wait_recv()
@@ -444,6 +451,11 @@
     rs_all.wait_recv()
     hand_all.wait_recv()
     total = jnp.sum(rs_recv[...] + hand_recv[...], axis=0)
+
+    def place_of(ref, i):
+        rows_at = pl.ds(pl.multiple_of(lax.rem(i // 2, 8) * 8, 8), 8)
+        return ref.at[i // 16, rows_at, pl.ds(pl.multiple_of(lax.rem(i, 2) * 128, 128), 128)]
+
     old = cb[
         2 * z + me // 16,
         pl.ds(pl.multiple_of(lax.rem(me // 2, 8) * 8, 8), 8),
@@ -451,13 +463,10 @@
     ]
     ag_send[...] = (total + prior_weight * old) / (count + prior_weight)
 
-    def send_ag(k, c):
-        j = peer(k)
-        copy_to(ag_send, ag_recv.at[me], ag_sem.at[0], ag_sem.at[1], j, z).start()
-        return c
-
-    lax.fori_loop(1, NL, send_ag, 0)
-    ag_recv[me] = ag_send[...]
+    for j in far_first():
+        copy_to(ag_send, place_of(newcb, me), ag_sem.at[0], ag_sem.at[1], j, z).start()
+    own_piece = pltpu.make_async_copy(ag_send, place_of(newcb, me), local_sem.at[3])
+    own_piece.start()
 
     et_all.wait_recv()
     rest = et_recv[...].reshape(NL, 128)
@@ -473,10 +482,7 @@
     err_out[...] = jnp.sum(jnp.where(belongs, picked, 0.0), axis=0, keepdims=True)
 
     ag_all.wait_recv()
-    for a in range(2):
-        for d in range(8):
-            for h in range(2):
-                newcb[a, d * 8 : (d + 1) * 8, h * 128 : (h + 1) * 128] = ag_recv[a * 16 + d * 2 + h]
+    own_piece.wait()
 
     copy_to(
         mt_send.at[pl.ds(0, 248)], mt_recv.at[pl.ds(0, 248)], meta_sem.at[0], meta_sem.at[1], me, z
@@ -528,7 +534,7 @@
             jax.ShapeDtypeStruct((1, ROWS), F32),
         ),
         in_specs=[pl.BlockSpec(memory_space=pltpu.SMEM), vmem, vmem, vmem, anywhere, anywhere, anywhere],
-        out_specs=(vmem, vmem),
+        out_specs=(anywhere, vmem),
         scratch_shapes=[
             pltpu.VMEM((ROWS, D), BF16),
             pltpu.VMEM((LISTS, D), BF16),
@@ -560,10 +566,9 @@
             pltpu.VMEM((NL, 8, 128), F32),
             pltpu.VMEM((NL, 8, 128), F32),
             pltpu.VMEM((8, 128), F32),
-            pltpu.VMEM((NL, 8, 128), F32),
             pltpu.VMEM((NL, 1, 128), F32),
             pltpu.VMEM((NL, 1, 128), F32),
-            dma((3,)),
+            dma((4,)),
             dma((2,)),
             dma((STEPS,)),
             dma((STEPS,)),

time: 58.2 us -> 57.4 us (0.986)
  Pallas kernels: 56.7 us -> 56 us
    pallas_call x1, Pallas kernels: 55.1 us -> 54.4 us  [body(): pl.pallas_call(kernel, out_shape=(jax.ShapeDtypeStruct((2, DS, K), F32),...]
where the time goes in v3:
time: 57.4 us; the launch traced here: 57.2 us
  Pallas kernels  56 us (98%)
  between operations  1.29 us (2%)
    pallas_call x1, Pallas kernels, body(): pl.pallas_call(kernel, out_shape=(jax.ShapeDtypeStruct((2, DS, K), F32),...  54.4 us
    pallas_call x1, Pallas kernels, body(): pl.pallas_call(hand_over, out_shape=(jax.ShapeDtypeStruct((2, DS, K), F32...  1.57 us

profile of v3, /device:TPU:1, one launch (start us, length us, event | category | flops | bytes accessed | tf_op | source)
XLA Modules:
  0.0 57.2 jit_solution(6775959243642611941)
XLA Ops:
  1.3 54.4 %shard_map.86 = (f32[2,64,256]{2,1,0:T(8,128)}, f32[1,256]{1,0:T(1,128)}) custom-call(s32[1]{0:T(128)S(6)} %copy.9.valid, s32[1,256]{1,0:T(1,128)} %bitcast.8, s32[1,256]{1,0:T(1,128)} %bitcast.9, s32[16,256]{1,0:T(8,128)} %bitcast.7, bf16[256,1024]{1,0:T(8,128)(2,1)} %rows_hbm.1, bf16[2048,1024]{1,0:T(8,128)(2,1)} %cent_hbm.1, f32[16,64,256]{2,1,0:T(8,128)} %bitcast.6), custom_call_target="tpu_custom_call" | custom-call | tf_op jit(solution)/shard_map/pallas_call | solution.py:530
  55.7 1.6 %shard_map.87 = (f32[2,64,256]{2,1,0:T(8,128)}, f32[1,256]{1,0:T(1,128)}) custom-call(f32[2,64,256]{2,1,0:T(8,128)} %get-tuple-element.6.newcb_in, f32[1,256]{1,0:T(1,128)} %get-tuple-element.7.err_in), custom_call_target="tpu_custom_call" | custom-call | tf_op jit(solution)/shard_map/pallas_call | solution.py:597

commit v4 on v3

--- a/solution.py
+++ b/solution.py
@@ -219,8 +219,7 @@
 
     def start(v, h):
         c = 2 * v + h
-        for k in range(1, NL):
-            j = peer(k)
+        for j in far_first():
             copy_to(
                 send.at[c, tile32(j)], recv.at[c, tile32(me)], data_ss.at[c], data_rs.at[c], j, z
             ).start()

time: 57.4 us -> 56.6 us (0.986)
  Pallas kernels: 56 us -> 55.1 us
    pallas_call x1, Pallas kernels: 54.4 us -> 53.6 us  [body(): pl.pallas_call(kernel, out_shape=(jax.ShapeDtypeStruct((2, DS, K), F32),...]
where the time goes in v4:
time: 56.6 us; the launch traced here: 56.4 us
  Pallas kernels  55.1 us (97%)
  between operations  1.29 us (2%)
    pallas_call x1, Pallas kernels, body(): pl.pallas_call(kernel, out_shape=(jax.ShapeDtypeStruct((2, DS, K), F32),...  53.6 us
    pallas_call x1, Pallas kernels, body(): pl.pallas_call(hand_over, out_shape=(jax.ShapeDtypeStruct((2, DS, K), F32...  1.57 us

profile of v4, /device:TPU:1, one launch (start us, length us, event | category | flops | bytes accessed | tf_op | source)
XLA Modules:
  0.0 56.4 jit_solution(3737923862446522345)
XLA Ops:
  1.3 53.6 %shard_map.86 = (f32[2,64,256]{2,1,0:T(8,128)}, f32[1,256]{1,0:T(1,128)}) custom-call(s32[1]{0:T(128)S(6)} %copy.9.valid, s32[1,256]{1,0:T(1,128)} %bitcast.8, s32[1,256]{1,0:T(1,128)} %bitcast.9, s32[16,256]{1,0:T(8,128)} %bitcast.7, bf16[256,1024]{1,0:T(8,128)(2,1)} %rows_hbm.1, bf16[2048,1024]{1,0:T(8,128)(2,1)} %cent_hbm.1, f32[16,64,256]{2,1,0:T(8,128)} %bitcast.6), custom_call_target="tpu_custom_call" | custom-call | tf_op jit(solution)/shard_map/pallas_call | solution.py:529
  54.8 1.6 %shard_map.87 = (f32[2,64,256]{2,1,0:T(8,128)}, f32[1,256]{1,0:T(1,128)}) custom-call(f32[2,64,256]{2,1,0:T(8,128)} %get-tuple-element.6.newcb_in, f32[1,256]{1,0:T(1,128)} %get-tuple-element.7.err_in), custom_call_target="tpu_custom_call" | custom-call | tf_op jit(solution)/shard_map/pallas_call | solution.py:596

commit v5 on v4

--- a/solution.py
+++ b/solution.py
@@ -225,12 +225,10 @@
             ).start()
         recv[c, tile32(me), :] = send[c, tile32(me), :]
 
-    def send_meta(k, c):
-        j = peer(k)
-        copy_to(mt_send.at[tile8(j)], mt_recv.at[tile8(me)], meta_sem.at[0], meta_sem.at[1], j, z).start()
-        return c
-
-    lax.fori_loop(1, NL, send_meta, 0)
+    for j in far_first():
+        copy_to(
+            mt_send.at[tile8(j)], mt_recv.at[tile8(me)], meta_sem.at[0], meta_sem.at[1], j, z
+        ).start()
     mt_recv[tile8(me), :] = mt_send[tile8(me), :]
 
 

time: 56.6 us -> 56 us (0.989)
    pallas_call x1, Pallas kernels: 53.6 us -> 53 us  [body(): pl.pallas_call(kernel, out_shape=(jax.ShapeDtypeStruct((2, DS, K), F32),...]
where the time goes in v5:
time: 56 us; the launch traced here: 55.8 us
  Pallas kernels  54.6 us (98%)
  between operations  1.29 us (2%)
    pallas_call x1, Pallas kernels, body(): pl.pallas_call(kernel, out_shape=(jax.ShapeDtypeStruct((2, DS, K), F32),...  53 us
    pallas_call x1, Pallas kernels, body(): pl.pallas_call(hand_over, out_shape=(jax.ShapeDtypeStruct((2, DS, K), F32...  1.57 us

profile of v5, /device:TPU:1, one launch (start us, length us, event | category | flops | bytes accessed | tf_op | source)
XLA Modules:
  0.0 55.8 jit_solution(1185497938393988710)
XLA Ops:
  1.3 53.0 %shard_map.86 = (f32[2,64,256]{2,1,0:T(8,128)}, f32[1,256]{1,0:T(1,128)}) custom-call(s32[1]{0:T(128)S(6)} %copy.9.valid, s32[1,256]{1,0:T(1,128)} %bitcast.8, s32[1,256]{1,0:T(1,128)} %bitcast.9, s32[16,256]{1,0:T(8,128)} %bitcast.7, bf16[256,1024]{1,0:T(8,128)(2,1)} %rows_hbm.1, bf16[2048,1024]{1,0:T(8,128)(2,1)} %cent_hbm.1, f32[16,64,256]{2,1,0:T(8,128)} %bitcast.6), custom_call_target="tpu_custom_call" | custom-call | tf_op jit(solution)/shard_map/pallas_call | solution.py:527
  54.3 1.6 %shard_map.87 = (f32[2,64,256]{2,1,0:T(8,128)}, f32[1,256]{1,0:T(1,128)}) custom-call(f32[2,64,256]{2,1,0:T(8,128)} %get-tuple-element.6.newcb_in, f32[1,256]{1,0:T(1,128)} %get-tuple-element.7.err_in), custom_call_target="tpu_custom_call" | custom-call | tf_op jit(solution)/shard_map/pallas_call | solution.py:594
